TPU v7x, 32 devices: a whole 2x2x4 slice. The times are simulated.
32 devices in a mesh: col: 16 (over z, y, x), row: 2 (over core).
Axes of the slice: x: 2, y: 2, z: 4, core: 2. Of those that a mesh axis runs over, the one named last changes fastest.
Arguments:
- top_rows: float32 [1792, 8192], P(None, ('col', 'row')), may hold values from -0.0625 to 0.0625
- lower_new: float32 [8192, 256], P(('col', 'row')), may hold values from -6 to 6
- block_order: int32 [32, 2], P(('col', 'row')), may hold values from 0 to 1, each once within a row
- corner: float32 [1792, 1792], P('row'), may hold values from -0.125 to 0.125
- target: float32 [1792, 256], P('row'), may hold values from -6 to 6
- coupling: float32 [128, 128], replicated, may hold values from -0.5 to 0.5
- top_right: float32 [14, 128, 128], P('row'), may hold values from -0.5 to 0.5
- top_left: float32 [14, 128, 128], P('row'), may hold values from -0.5 to 0.5
- top_values: float32 [14, 128], P('row'), may hold values from 0.5 to 2
- new_right: float32 [2, 128, 128], replicated, may hold values from -0.5 to 0.5
- new_left: float32 [2, 128, 128], replicated, may hold values from -0.5 to 0.5
- new_values: float32 [2, 128], replicated, may hold values from 0.5 to 2
Outputs:
- solution: float32 [1792, 256], P('row')
Inputs may be any that keep to these rules, and one draw needn't show every extreme that they name: Each row of block_order is an ordering of 0 to 1.
All inputs are finite; a program needn't handle non-finite values.
Results may differ from a plain program's by a relative error of at most 0.0001.
Values sent between devices are 32-bit elements; how exact they have to be, the bound alone decides.
No kernel may reach another device: no remote copies, remote signals or barrier semaphores. Data moves between devices by JAX's collectives and lax.ppermute only.
A program may use at most 64 MiB of HBM per device.

v0:
```python
import jax
import jax.numpy as jnp
from jax import lax
from jax.sharding import PartitionSpec as P

PRECISION = lax.Precision.HIGHEST


def shifted(block, axis, distance):
    devices = range(lax.axis_size(axis))
    route = [(i - distance, i) for i in devices if i - distance in devices]
    return lax.ppermute(block, axis, route)


def solve_block(right_side, left_right, left_left, left_values, col_right, col_left, col_values):
    rotated = jnp.dot(
        jnp.dot(left_left, right_side, precision=PRECISION), col_right, precision=PRECISION
    )
    rotated = rotated / (left_values[:, None] + col_values[None, :])
    return jnp.dot(jnp.dot(left_right, rotated, precision=PRECISION), col_left, precision=PRECISION)


def sweep(
    right_side,
    own_block,
    top_right,
    top_left,
    top_values,
    col_right,
    col_left,
    col_values,
    earlier,
    coupling,
):
    block_size = top_right.shape[1]
    solved = []
    for position in range(top_right.shape[0] - 1, -1, -1):
        offset = position * block_size
        current = right_side[offset : offset + block_size]
        if earlier is not None:
            current = current - jnp.dot(
                earlier[offset : offset + block_size], coupling, precision=PRECISION
            )
        result = solve_block(
            current,
            top_right[position],
            top_left[position],
            top_values[position],
            col_right,
            col_left,
            col_values,
        )
        right_side = right_side - jnp.dot(
            own_block[:, offset : offset + block_size], result, precision=PRECISION
        )
        solved.append(result)
    return jnp.concatenate(solved[::-1], axis=0)


def shards(
    top_rows,
    lower_new,
    block_order,
    corner,
    target,
    coupling,
    top_right,
    top_left,
    top_values,
    new_right,
    new_left,
    new_values,
):
    block_size = coupling.shape[0]
    groups = block_order.shape[1]
    lower_blocks = lower_new.reshape(groups, block_size, 2 * block_size)
    paired = jnp.take(lower_blocks, block_order[0], axis=0).reshape(
        groups * block_size, 2 * block_size
    )
    partial_value = jnp.dot(top_rows, paired, precision=PRECISION)
    half_rows = target.shape[0]
    row_index = lax.axis_index("row")
    own_half = lax.psum_scatter(partial_value, "row", scatter_dimension=0, tiled=True)
    own_rows = lax.psum(own_half, "col")
    right_side = target - own_rows
    total_cols = corner.shape[1]
    row_block = (row_index * half_rows + jnp.arange(half_rows)) // block_size
    col_block = jnp.arange(total_cols) // block_size
    masked = jnp.where(row_block[:, None] < col_block[None, :], corner, jnp.zeros_like(corner))
    own_block = lax.dynamic_slice_in_dim(masked, row_index * half_rows, half_rows, 1)
    next_start = jnp.minimum(row_index + 1, lax.axis_size("row") - 1) * half_rows
    next_block = lax.dynamic_slice_in_dim(masked, next_start, half_rows, 1)
    left_side = right_side[:, :block_size]
    right_part = right_side[:, block_size:]
    first_left = sweep(
        left_side,
        own_block,
        top_right,
        top_left,
        top_values,
        new_right[0],
        new_left[0],
        new_values[0],
        None,
        coupling,
    )
    first_right = sweep(
        right_part,
        own_block,
        top_right,
        top_left,
        top_values,
        new_right[1],
        new_left[1],
        new_values[1],
        first_left,
        coupling,
    )
    below_left, below_right = shifted((first_left, first_right), "row", -1)
    final_left = sweep(
        left_side - jnp.dot(next_block, below_left, precision=PRECISION),
        own_block,
        top_right,
        top_left,
        top_values,
        new_right[0],
        new_left[0],
        new_values[0],
        None,
        coupling,
    )
    final_right = sweep(
        right_part - jnp.dot(next_block, below_right, precision=PRECISION),
        own_block,
        top_right,
        top_left,
        top_values,
        new_right[1],
        new_left[1],
        new_values[1],
        final_left,
        coupling,
    )
    return jnp.concatenate([final_left, final_right], axis=1)


def solution(mesh):
    placed = (
        P(None, ("col", "row")),
        P(("col", "row"), None),
        P(("col", "row"), None),
        P("row", None),
        P("row", None),
        P(),
        P("row", None, None),
        P("row", None, None),
        P("row", None),
        P(),
        P(),
        P(),
    )
    return jax.shard_map(
        shards, mesh=mesh, in_specs=placed, out_specs=P("row", None), check_vma=False
    )
```

profile of v0, /device:TPU:1, one launch (start us, length us, event | category | flops | bytes accessed | tf_op | source)
XLA Modules:
  0.0 218.7 jit_solution(16706956188284991691)
XLA Ops:
  6.6 0.8 fusion.390
  7.4 0.7 compare_and_fusion
  8.2 1.5 gather_fusion
  9.8 4.3 %convolution_bitcast_fusion = f32[1792,256]{0,1:T(8,128)} fusion(f32[256,256]{1,0:T(8,128)S(1)} %bitcast_select_fusion, f32[1792,256]{1,0:T(8,128)S(1)} %copy-done), kind=kOutput, calls=%fused_computation.6 | convolution fusion | flops 1409286144 | bytes 3932160 | tf_op jit(solution)/shard_map/dot_general | solution.py:80
  14.5 1.2 copy.13
  15.8 10.4 %reduce-scatter.2.cloned.1.call-done = f32[896,256]{0,1:T(8,128)} async-done(((f32[1792,256]{0,1:T(8,128)}), f32[896,256]{0,1:T(8,128)}) %reduce-scatter.2.cloned.1.call-update) | async-done | bytes 917520 | tf_op jit(solution)/shard_map/reduce_scatter | solution.py:83
  26.2 6.1 %compare_select_fusion = f32[896,1792]{1,0:T(8,128)} fusion(f32[896,1792]{1,0:T(8,128)} %param.15, s32[1792]{0:T(1024)S(1)} %add_select_fusion, s32[896]{0:T(1024)S(1)} %add_select_fusion.1), kind=kLoop, calls=%fused_computation.1 | loop fusion | flops 3211264 | bytes 12855808 | tf_op jit(solution)/shard_map/jit(_where)/select_n | solution.py:89
  32.4 109.5 %all-reduce.2.cloned.1.call-done = f32[896,256]{0,1:T(8,128)} async-done(((f32[896,256]{0,1:T(8,128)}), f32[896,256]{0,1:T(8,128)}) %all-reduce.2.cloned.1.call-update) | async-done | bytes 917520 | tf_op jit(solution)/shard_map/psum | solution.py:84
  141.9 1.7 sub.135
  144.8 1.7 convolution_subtract_fusion.19
  147.6 1.7 convolution_subtract_fusion.18
  154.0 0.6 convolution_subtract_fusion.15
  157.6 5.0 %collective-permute-start = (f32[896,128]{1,0:T(8,128)S(1)}, f32[896,128]{1,0:T(8,128)S(1)}, u32[]{:S(2)}, u32[]{:S(2)}) collective-permute-start(f32[896,128]{1,0:T(8,128)S(1)} %constant_dynamic-update-slice_fusion), channel_id=1, source_target_pairs={{1,0},{3,2},{5,4},{7,6},{9,8},{11,10},{13,12},{15,14},{17,16},{19,... | collective-permute-start | bytes 1376264 | tf_op jit(solution)/shard_map/ppermute | solution.py:12
  164.1 0.6 convolution_subtract_fusion.9
  166.1 0.6 convolution_subtract_fusion.8
  172.4 0.6 convolution_subtract_fusion.5
  176.6 1.5 collective-permute-start.1
  178.1 3.1 %fusion.4 = f32[896,128]{0,1:T(8,128)S(1)} fusion(f32[896,128]{1,0:T(8,128)S(1)} %collective-permute-done, f32[896,1792]{1,0:T(8,128)S(1)} %copy-done.1, s32[]{:T(128)S(6)} %select_n.55, f32[896,256]{0,1:T(8,128)S(1)} %sub.135), kind=kOutput, calls=%fused_computation.7 | convolution fusion | flops 1233240064 | bytes 4587524 | tf_op jit(solution)/shard_map/dot_general | solution.py:121
  182.4 0.6 convolution_subtract_fusion.14
  193.5 3.4 %fusion.7 = f32[896,128]{0,1:T(8,128)S(1)} fusion(f32[896,128]{1,0:T(8,128)S(1)} %collective-permute-done.1, f32[896,1792]{1,0:T(8,128)S(1)} %copy-done.1, s32[]{:T(128)S(6)} %select_n.55, f32[896,256]{0,1:T(8,128)S(1)} %sub.135), kind=kOutput, calls=%fused_computation.8 | convolution fusion | flops 1233240064 | bytes 4587524 | tf_op jit(solution)/shard_map/dot_general | solution.py:133
  200.1 0.6 convolution_subtract_fusion.3
  202.2 0.6 convolution_subtract_fusion.2
  206.3 0.6 convolution_subtract_fusion
  210.6 1.0 pad_maximum_fusion
  (197 shorter events, 45.1 us)
Async XLA Ops:
  6.5 3.2 %copy-start = (f32[1792,256]{1,0:T(8,128)S(1)}, f32[1792,256]{1,0:T(8,128)}, u32[]{:S(2)}) copy-start(f32[1792,256]{1,0:T(8,128)} %param.12) | copy-start | bytes 5505028
  6.5 8.0 %copy-start.6 = (f32[896,256]{1,0:T(8,128)S(1)}, f32[896,256]{1,0:T(8,128)}, u32[]{:S(2)}) copy-start(f32[896,256]{1,0:T(8,128)} %param.16) | copy-start | bytes 2752516
  6.5 9.2 %copy-start.8 = (f32[2,128]{1,0:T(2,128)S(1)}, f32[2,128]{1,0:T(2,128)}, u32[]{:S(2)}) copy-start(f32[2,128]{1,0:T(2,128)} %param.23) | copy-start | bytes 3076
  6.5 9.2 %copy-start.7 = (f32[7,128]{1,0:T(8,128)S(1)}, f32[7,128]{1,0:T(8,128)}, u32[]{:S(2)}) copy-start(f32[7,128]{1,0:T(8,128)} %param.20) | copy-start | bytes 10756
  6.5 19.6 %reduce-scatter.2.cloned.1.call-start = ((), (), s32[]{:S(2)}) async-start(), calls=%async_computation.1 | async-start | bytes 2752512 | tf_op jit(solution)/shard_map/reduce_scatter | solution.py:83
  14.2 127.7 %all-reduce.2.cloned.1.call-start = ((), (), s32[]{:S(2)}) async-start(), calls=%async_computation.2 | async-start | bytes 1835008 | tf_op jit(solution)/shard_map/psum | solution.py:84
  26.2 117.4 %copy-start.4 = (f32[7,128,128]{2,1,0:T(8,128)S(1)}, f32[7,128,128]{2,1,0:T(8,128)}, u32[]{:S(2)}) copy-start(f32[7,128,128]{2,1,0:T(8,128)} %param.19) | copy-start | bytes 1376260
  26.2 117.6 %copy-start.9 = (f32[2,128,128]{2,1,0:T(8,128)S(1)}, f32[2,128,128]{2,1,0:T(8,128)}, u32[]{:S(2)}) copy-start(f32[2,128,128]{2,1,0:T(8,128)} %param.21) | copy-start | bytes 393220
  26.2 117.9 %copy-start.5 = (f32[7,128,128]{2,1,0:T(8,128)S(1)}, f32[7,128,128]{2,1,0:T(8,128)}, u32[]{:S(2)}) copy-start(f32[7,128,128]{2,1,0:T(8,128)} %param.18) | copy-start | bytes 1376260
  26.2 118.2 %copy-start.2 = (f32[2,128,128]{2,1,0:T(8,128)S(1)}, f32[2,128,128]{2,1,0:T(8,128)}, u32[]{:S(2)}) copy-start(f32[2,128,128]{2,1,0:T(8,128)} %param.22) | copy-start | bytes 393220
  141.9 8.5 %copy-start.1 = (f32[896,1792]{1,0:T(8,128)S(1)}, f32[896,1792]{1,0:T(8,128)}, u32[]{:S(2)}) copy-start(f32[896,1792]{1,0:T(8,128)} %compare_select_fusion) | copy-start | bytes 19267588
  146.4 16.2 %copy-start.3 = (f32[128,128]{1,0:T(8,128)S(1)}, f32[128,128]{1,0:T(8,128)}, u32[]{:S(2)}) copy-start(f32[128,128]{1,0:T(8,128)} %param.17) | copy-start | bytes 196612
  157.6 20.5 %collective-permute-start = (f32[896,128]{1,0:T(8,128)S(1)}, f32[896,128]{1,0:T(8,128)S(1)}, u32[]{:S(2)}, u32[]{:S(2)}) collective-permute-start(f32[896,128]{1,0:T(8,128)S(1)} %constant_dynamic-update-slice_fusion), channel_id=1, source_target_pairs={{1,0},{3,2},{5,4},{7,6},{9,8},{11,10},{13,12},{15,14},{17,16},{19,... | collective-permute-start | bytes 1376264 | tf_op jit(solution)/shard_map/ppermute | solution.py:12
  176.6 16.9 %collective-permute-start.1 = (f32[896,128]{1,0:T(8,128)S(1)}, f32[896,128]{1,0:T(8,128)S(1)}, u32[]{:S(2)}, u32[]{:S(2)}) collective-permute-start(f32[896,128]{1,0:T(8,128)S(1)} %constant_dynamic-update-slice_fusion.14), channel_id=1, source_target_pairs={{1,0},{3,2},{5,4},{7,6},{9,8},{11,10},{13,12},{15,14},{17,16},{19,... | collective-permute-start | bytes 1376264 | tf_op jit(solution)/shard_map/ppermute | solution.py:12
Sparse Core Ops, SparseCore 0:
  14.3 11.8 reduce-scatter.1
  31.4 110.3 all-reduce.1
where the time goes:
time: 222 us; the launch traced here: 219 us
  waiting for transfers between devices  120 us (54%)
  matrix products  63.4 us (29%)
  between operations  15 us (7%)
  other arithmetic  10.5 us (5%)
  starting transfers between devices  6.82 us (3%)
  local copies, waits for them, and re-layouts  3.05 us (1%)
    psum x1, waiting for transfers between devices, shards(): own_rows = lax.psum(own_half, 'col')  109 us
    dot_general x24, matrix products, sweep(): jnp.dot(own_block[:, offset:offset + block_size], result, precision=PRECI...  17.1 us
    reduce_scatter x1, waiting for transfers between devices, shards(): lax.psum_scatter(partial_value, 'row', scatter_dimension=0, tiled=True)  10.4 us
    dot_general x28, matrix products, solve_block(): jnp.dot(jnp.dot(left_left, right_side, precision=PRECISION), col_right, p...  8.09 us
    dot_general x28, matrix products, solve_block(): jnp.dot(left_right, rotated, precision=PRECISION)  7.97 us
    dot_general x28, matrix products, solve_block(): jnp.dot(jnp.dot(left_right, rotated, precision=PRECISION), col_left, prec...  7.97 us
    dot_general x28, matrix products, solve_block(): jnp.dot(left_left, right_side, precision=PRECISION)  7.48 us
    ppermute x2, starting transfers between devices, shifted(): return lax.ppermute(block, axis, route)  6.45 us
  transfers between devices with their start and end apart: 4, of which 2 were waited for; matrix products, arithmetic and copies ran while one was open for 17% of the time, Pallas kernels for 0%

commit v1 on v0

--- a/solution.py
+++ b/solution.py
@@ -81,7 +81,7 @@
     half_rows = target.shape[0]
     row_index = lax.axis_index("row")
     own_half = lax.psum_scatter(partial_value, "row", scatter_dimension=0, tiled=True)
-    own_rows = lax.psum(own_half, "col")
+    own_rows = jnp.sum(lax.all_gather(own_half, "col"), axis=0)
     right_side = target - own_rows
     total_cols = corner.shape[1]
     row_block = (row_index * half_rows + jnp.arange(half_rows)) // block_size

time: 222 us -> 297 us (1.34)
  waiting for transfers between devices: 120 us -> 182 us
  local copies, waits for them, and re-layouts: 3.05 us -> 15.1 us
  other arithmetic: 10.5 us -> 17.8 us
  matrix products: 63.4 us -> 59.7 us
    all_gather x0 -> x1, waiting for transfers between devices: none -> 170 us  [shards(): own_rows = jnp.sum(lax.all_gather(own_half, 'col'), axis=0)]
    psum x1 -> x0, waiting for transfers between devices: 109 us -> none  [shards(): own_rows = lax.psum(own_half, 'col')]
    unnamed x41, local copies, waits for them, and re-layouts: 1.42 us -> 13.1 us
    reduce_sum x0 -> x1, other arithmetic: none -> 7.66 us  [shards(): own_rows = jnp.sum(lax.all_gather(own_half, 'col'), axis=0)]
  transfers between devices with their start and end apart: 4 -> 4, of which waited for: 2 -> 2; matrix products, arithmetic and copies ran while one was open for 17% -> 11% of each run, Pallas kernels for 0% -> 0%
where the time goes in v1:
time: 297 us; the launch traced here: 294 us
  waiting for transfers between devices  182 us (61%)
  matrix products  59.7 us (20%)
  other arithmetic  17.8 us (6%)
  between operations  15.2 us (5%)
  local copies, waits for them, and re-layouts  15.1 us (5%)
  starting transfers between devices  4.48 us (2%)
    all_gather x1, waiting for transfers between devices, shards(): own_rows = jnp.sum(lax.all_gather(own_half, 'col'), axis=0)  170 us
    dot_general x24, matrix products, sweep(): jnp.dot(own_block[:, offset:offset + block_size], result, precision=PRECI...  14.4 us
    unnamed x41, local copies, waits for them, and re-layouts  13.1 us
    reduce_scatter x1, waiting for transfers between devices, shards(): lax.psum_scatter(partial_value, 'row', scatter_dimension=0, tiled=True)  11.8 us
    dot_general x28, matrix products, solve_block(): jnp.dot(jnp.dot(left_right, rotated, precision=PRECISION), col_left, prec...  8.36 us
    dot_general x28, matrix products, solve_block(): jnp.dot(jnp.dot(left_left, right_side, precision=PRECISION), col_right, p...  8.02 us
    dot_general x28, matrix products, solve_block(): jnp.dot(left_left, right_side, precision=PRECISION)  7.95 us
    dot_general x28, matrix products, solve_block(): jnp.dot(left_right, rotated, precision=PRECISION)  7.95 us
  transfers between devices with their start and end apart: 4, of which 2 were waited for; matrix products, arithmetic and copies ran while one was open for 11% of the time, Pallas kernels for 0%

profile of v1, /device:TPU:1, one launch (start us, length us, event | category | flops | bytes accessed | tf_op | source)
XLA Modules:
  0.0 294.0 jit_solution(698916795098454297)
XLA Ops:
  6.5 0.8 fusion.390
  7.3 0.7 compare_and_fusion
  8.1 1.5 gather_fusion
  9.7 4.3 %convolution_bitcast_fusion = f32[1792,256]{0,1:T(8,128)} fusion(f32[256,256]{1,0:T(8,128)S(1)} %bitcast_select_fusion, f32[1792,256]{1,0:T(8,128)S(1)} %copy-done), kind=kOutput, calls=%fused_computation.7 | convolution fusion | flops 1409286144 | bytes 3932160 | tf_op jit(solution)/shard_map/dot_general | solution.py:80
  14.3 11.8 %reduce-scatter.2.cloned.1.call-done = f32[896,256]{0,1:T(8,128)} async-done(((f32[1792,256]{0,1:T(8,128)}), f32[896,256]{0,1:T(8,128)}) %reduce-scatter.2.cloned.1.call-update) | async-done | bytes 917520 | tf_op jit(solution)/shard_map/reduce_scatter | solution.py:83
  26.2 6.0 %compare_select_fusion = f32[896,1792]{1,0:T(8,128)} fusion(f32[896,1792]{1,0:T(8,128)} %param.15, s32[1792]{0:T(1024)S(1)} %add_select_fusion, s32[896]{0:T(1024)S(1)} %add_select_fusion.1), kind=kLoop, calls=%fused_computation.2 | loop fusion | flops 3211264 | bytes 12855808 | tf_op jit(solution)/shard_map/jit(_where)/select_n | solution.py:89
  32.2 169.9 %all-gather.3.cloned.1.call-done = f32[14336,256]{0,1:T(8,128)} async-done(((f32[896,256]{0,1:T(8,128)}), f32[14336,256]{0,1:T(8,128)}) %all-gather.3.cloned.1.call-update) | async-done | bytes 14680080 | tf_op jit(solution)/shard_map/all_gather | solution.py:84
  202.2 12.9 %copy.14 = f32[32,8,16,896]{3,2,1,0:T(8,128)} copy(f32[32,8,16,896]{3,1,2,0:T(8,128)} %bitcast.435) | data formatting | bytes 29360128
  215.1 7.7 %bitcast_reduce_fusion = f32[896,256]{0,1:T(8,128)S(1)} fusion(f32[32,8,16,896]{3,2,1,0:T(8,128)} %copy.14), kind=kLoop, calls=%fused_computation.1 | loop fusion | flops 3440640 | bytes 15597568 | tf_op jit(solution)/shard_map/reduce_sum | solution.py:84
  223.1 1.4 sub.135
  225.8 1.5 convolution_subtract_fusion.19
  228.5 1.5 convolution_subtract_fusion.18
  232.9 0.5 convolution_subtract_fusion.16
  234.3 0.7 fusion.209
  238.5 2.8 collective-permute-start
  254.2 1.5 collective-permute-start.1
  255.7 2.8 fusion.4
  259.6 0.5 convolution_subtract_fusion.14
  266.6 0.5 convolution_subtract_fusion.10
  270.0 3.0 %fusion.7 = f32[896,128]{1,0:T(8,128)S(1)} fusion(f32[896,128]{1,0:T(8,128)S(1)} %collective-permute-done.1, f32[896,1792]{1,0:T(8,128)S(1)} %copy-done.2, s32[]{:T(128)S(6)} %select_n.55, f32[896,256]{1,0:T(8,128)S(1)} %sub.135), kind=kOutput, calls=%fused_computation.9 | convolution fusion | flops 1233240064 | bytes 4587524 | tf_op jit(solution)/shard_map/dot_general | solution.py:133
  274.2 0.5 convolution_subtract_fusion.4
  276.1 0.5 convolution_subtract_fusion.3
  281.8 0.5 convolution_subtract_fusion
  285.8 1.0 pad_maximum_fusion
  (198 shorter events, 43.7 us)
Async XLA Ops:
  6.5 3.2 %copy-start = (f32[1792,256]{1,0:T(8,128)S(1)}, f32[1792,256]{1,0:T(8,128)}, u32[]{:S(2)}) copy-start(f32[1792,256]{1,0:T(8,128)} %param.12) | copy-start | bytes 5505028
  6.5 19.6 %copy-start.8 = (f32[2,128]{1,0:T(2,128)S(1)}, f32[2,128]{1,0:T(2,128)}, u32[]{:S(2)}) copy-start(f32[2,128]{1,0:T(2,128)} %param.23) | copy-start | bytes 3076
  6.5 19.6 %copy-start.7 = (f32[7,128]{1,0:T(8,128)S(1)}, f32[7,128]{1,0:T(8,128)}, u32[]{:S(2)}) copy-start(f32[7,128]{1,0:T(8,128)} %param.20) | copy-start | bytes 10756
  6.5 19.6 %reduce-scatter.2.cloned.1.call-start = ((), (), s32[]{:S(2)}) async-start(), calls=%async_computation.1 | async-start | bytes 2752512 | tf_op jit(solution)/shard_map/reduce_scatter | solution.py:83
  14.1 188.1 %all-gather.3.cloned.1.call-start = ((), (), s32[]{:S(2)}) async-start(), calls=%async_computation.2 | async-start | bytes 15597568 | tf_op jit(solution)/shard_map/all_gather | solution.py:84
  215.1 9.4 %copy-start.5 = (f32[7,128,128]{2,1,0:T(8,128)S(1)}, f32[7,128,128]{2,1,0:T(8,128)}, u32[]{:S(2)}) copy-start(f32[7,128,128]{2,1,0:T(8,128)} %param.19) | copy-start | bytes 1376260
  215.1 9.7 %copy-start.9 = (f32[2,128,128]{2,1,0:T(8,128)S(1)}, f32[2,128,128]{2,1,0:T(8,128)}, u32[]{:S(2)}) copy-start(f32[2,128,128]{2,1,0:T(8,128)} %param.21) | copy-start | bytes 393220
  215.1 10.1 %copy-start.6 = (f32[7,128,128]{2,1,0:T(8,128)S(1)}, f32[7,128,128]{2,1,0:T(8,128)}, u32[]{:S(2)}) copy-start(f32[7,128,128]{2,1,0:T(8,128)} %param.18) | copy-start | bytes 1376260
  215.1 10.3 %copy-start.3 = (f32[2,128,128]{2,1,0:T(8,128)S(1)}, f32[2,128,128]{2,1,0:T(8,128)}, u32[]{:S(2)}) copy-start(f32[2,128,128]{2,1,0:T(8,128)} %param.22) | copy-start | bytes 393220
  223.1 8.1 %copy-start.2 = (f32[896,1792]{1,0:T(8,128)S(1)}, f32[896,1792]{1,0:T(8,128)}, u32[]{:S(2)}) copy-start(f32[896,1792]{1,0:T(8,128)} %compare_select_fusion) | copy-start | bytes 19267588
  227.3 14.0 %copy-start.4 = (f32[128,128]{1,0:T(8,128)S(1)}, f32[128,128]{1,0:T(8,128)}, u32[]{:S(2)}) copy-start(f32[128,128]{1,0:T(8,128)} %param.17) | copy-start | bytes 196612
  238.5 17.2 %collective-permute-start = (f32[896,128]{1,0:T(8,128)S(1)}, f32[896,128]{1,0:T(8,128)S(1)}, u32[]{:S(2)}, u32[]{:S(2)}) collective-permute-start(f32[896,128]{1,0:T(8,128)S(1)} %constant_dynamic-update-slice_fusion), channel_id=1, source_target_pairs={{1,0},{3,2},{5,4},{7,6},{9,8},{11,10},{13,12},{15,14},{17,16},{19,... | collective-permute-start | bytes 1376264 | tf_op jit(solution)/shard_map/ppermute | solution.py:12
  254.2 15.8 %collective-permute-start.1 = (f32[896,128]{1,0:T(8,128)S(1)}, f32[896,128]{1,0:T(8,128)S(1)}, u32[]{:S(2)}, u32[]{:S(2)}) collective-permute-start(f32[896,128]{1,0:T(8,128)S(1)} %constant_dynamic-update-slice_fusion.14), channel_id=1, source_target_pairs={{1,0},{3,2},{5,4},{7,6},{9,8},{11,10},{13,12},{15,14},{17,16},{19,... | collective-permute-start | bytes 1376264 | tf_op jit(solution)/shard_map/ppermute | solution.py:12
  277.7 9.2 %copy-start.1 = (f32[1792,256]{1,0:T(8,128)S(1)}, f32[1792,256]{1,0:T(8,128)}, u32[]{:S(2)}) copy-start(f32[1792,256]{1,0:T(8,128)} %param.12) | copy-start | bytes 5505028
Sparse Core Ops, SparseCore 0:
  14.2 11.8 reduce-scatter.1
  28.8 173.3 all-gather.2
